TPU v7x, 512 devices: a whole 4x4x16 slice. The times are simulated.
512 devices in a mesh: batch: 64 (over z, y), proto: 8 (over x, core).
Axes of the slice: x: 4, y: 4, z: 16, core: 2. Of those that a mesh axis runs over, the one named last changes fastest.
Arguments:
- embeddings: bfloat16 [65536, 256], P('batch'), as said below
- prototypes: bfloat16 [16384, 256], P('proto'), as said below
- partner: int32 [65536], P('batch'), may hold values from 0 to 65535, as said below
Outputs:
- emb_grad: float32 [65536, 256], P('batch')
- proto_grad: float32 [16384, 256], P('proto')
Inputs may be any that keep to these rules, and one draw needn't show every extreme that they name: partner[partner[b]] == b for every view b, and partner[b] lies in the aligned block of 1024 views whose block index differs from that of b by 32. `embeddings`: no row is zero. `prototypes`: no row is zero.
All inputs are finite; a program needn't handle non-finite values.
Results may differ from a plain program's by a relative error of at most 0.0016.
Values may be sent and summed in bfloat16 or wider, within the bound.
No kernel may reach another device: no remote copies, remote signals or barrier semaphores. Data moves between devices by JAX's collectives and lax.ppermute only.
A program may use at most 64 MiB of HBM per device.

v0:
```python
import jax
import jax.numpy as jnp
from jax import lax
from jax.sharding import PartitionSpec as P

ITERS = 3
epsilon_code = 0.05
sharpness_divisor = 0.1
norm_floor = 1e-06


def shifted(value, axis, steps):
    count = lax.axis_size(axis)
    pairs = [(source, (source + steps) % count) for source in range(count)]
    return lax.ppermute(value, axis, pairs)


def unit_rows(values):
    wide = values.astype(jnp.float32)
    scale = lax.rsqrt(jnp.mean(wide * wide, axis=1, keepdims=True) + norm_floor) / jnp.sqrt(
        jnp.float32(wide.shape[1])
    )
    return (wide * scale, scale)


def norm_back(upstream, units, scale):
    return scale * (upstream - units * jnp.sum(units * upstream, axis=1, keepdims=True))


def contract_rows(left, right):
    return lax.dot_general(
        left, right, (((0,), (0,)), ((), ())), preferred_element_type=jnp.float32
    )


def body(embeddings, prototypes, partner):
    view_units, view_scale = unit_rows(embeddings)
    proto_units, proto_scale = unit_rows(prototypes)
    views = view_units.astype(jnp.bfloat16)
    protos = proto_units.astype(jnp.bfloat16)
    row_count = views.shape[0]
    links = jnp.remainder(partner, row_count)
    separation_measure = lax.axis_size("batch") // 2
    centroid_raw_affinities = jnp.dot(views, protos.T, preferred_element_type=jnp.float32)
    kernel = jnp.exp(centroid_raw_affinities / epsilon_code)

    def column_scale_of(weight):
        column_part = jnp.sum(weight[:, None] * kernel, axis=0)
        return 1.0 / lax.psum(column_part, "batch")

    weight = jnp.ones((row_count,), jnp.float32)
    for sweep in range(ITERS - 1):
        column_scale = column_scale_of(weight)
        row_part = jnp.sum(kernel * column_scale[None, :], axis=1)
        weight = 1.0 / lax.psum(row_part, "proto")
    column_scale = column_scale_of(weight)
    tempered_affinities = jnp.exp(centroid_raw_affinities / sharpness_divisor)
    soft_part = jnp.sum(tempered_affinities, axis=1)
    dispersion_width = kernel * column_scale[None, :]
    line_aggregate, soft_total = lax.psum((jnp.sum(dispersion_width, axis=1), soft_part), "proto")
    balanced_transport_labels = (dispersion_width * (1.0 / line_aggregate)[:, None]).astype(
        jnp.bfloat16
    )
    received_pieces = shifted(balanced_transport_labels, "batch", separation_measure)
    centroid_agreement = received_pieces[links]
    estimated_likelihood = tempered_affinities * (1.0 / soft_total)[:, None]
    logit_gradient = (
        (estimated_likelihood - centroid_agreement.astype(jnp.float32)) / sharpness_divisor
    ).astype(jnp.bfloat16)
    view_part = jnp.dot(logit_gradient, protos, preferred_element_type=jnp.float32)
    view_upstream = lax.psum(view_part, "proto")
    emb_grad = norm_back(view_upstream, view_units, view_scale)
    proto_upstream = lax.psum(contract_rows(logit_gradient, views), "batch")
    proto_grad = norm_back(proto_upstream, proto_units, proto_scale)
    return (emb_grad, proto_grad)


def solution(mesh):
    return jax.shard_map(
        body,
        mesh=mesh,
        in_specs=(P("batch", None), P("proto", None), P("batch")),
        out_specs=(P("batch", None), P("proto", None)),
        check_vma=False,
    )
```

profile of v0, /device:TPU:2, one launch (start us, length us, event | category | flops | bytes accessed | tf_op | source)
XLA Modules:
  0.0 1267.4 jit_solution(6247067676049251214)
XLA Ops:
  7.2 0.0 all-reduce.4.cloned.1.call-start
  7.2 1.6 fusion.8
  8.8 1.3 fusion.15
  10.1 6.3 fusion.4
  16.3 151.9 %psum.64 = f32[2048]{0:T(1024)S(1)} all-reduce(f32[2048]{0:T(1024)S(1)} %get-tuple-element.6), channel_id=1, replica_groups=mesh['batch'=64,'proto'=8] {'batch'}, use_global_device_ids=true, to_apply=%region_5.6 | all-reduce | flops 2048 | bytes 16384 | tf_op jit(solution)/shard_map/psum | solution.py:49
  168.3 5.1 fusion
  173.4 10.0 psum.65
  183.4 4.3 multiply_reduce_fusion.2
  187.7 140.0 %psum.66 = f32[2048]{0:T(1024)S(1)} all-reduce(f32[2048]{0:T(1024)S(1)} %multiply_reduce_fusion.2), channel_id=1, replica_groups=mesh['batch'=64,'proto'=8] {'batch'}, use_global_device_ids=true, to_apply=%region_9.10 | all-reduce | flops 2048 | bytes 16384 | tf_op jit(solution)/shard_map/psum | solution.py:49
  327.8 4.8 multiply_reduce_fusion.1
  332.6 11.9 psum.67
  344.5 4.3 multiply_reduce_fusion
  348.8 142.1 %psum.68 = f32[2048]{0:T(1024)S(1)} all-reduce(f32[2048]{0:T(1024)S(1)} %multiply_reduce_fusion), channel_id=1, replica_groups=mesh['batch'=64,'proto'=8] {'batch'}, use_global_device_ids=true, to_apply=%region_13.14 | all-reduce | flops 2048 | bytes 16384 | tf_op jit(solution)/shard_map/psum | solution.py:49
  490.9 4.8 multiply_reduce_fusion.4
  495.8 12.6 all-reduce
  508.4 4.4 multiply_convert_fusion.1
  512.8 6.5 collective-permute-start
  519.4 293.3 %collective-permute-done = bf16[1024,2048]{1,0:T(8,128)(2,1)} collective-permute-done((bf16[1024,2048]{1,0:T(8,128)(2,1)S(1)}, bf16[1024,2048]{1,0:T(8,128)(2,1)}, u32[]{:S(2)}, u32[]{:S(2)}) %collective-permute-start) | collective-permute-done | bytes 4194336 | tf_op jit(solution)/shard_map/ppermute | solution.py:15
  812.7 11.6 gather_fusion
  824.2 6.1 multiply_convert_fusion
  830.3 1.9 copy-done.2
  832.2 2.3 fusion.16
  834.6 0.0 all-reduce.4.cloned.1.call-update
  834.6 0.0 all-reduce.6.cloned.1.call-start
  834.7 5.0 fusion.20
  839.7 0.0 all-reduce.6.cloned.1.call-update
  839.7 131.9 %all-reduce.4.cloned.1.call-done = f32[1024,256]{1,0:T(8,128)} async-done(((f32[1024,256]{1,0:T(8,128)}), f32[1024,256]{1,0:T(8,128)}) %all-reduce.4.cloned.1.call-update) | async-done | bytes 1048592 | tf_op jit(solution)/shard_map/psum | solution.py:71
  971.6 1.6 fusion.12
  973.2 2.5 fusion.14
  975.7 279.7 %all-reduce.6.cloned.1.call-done = f32[2048,256]{1,0:T(8,128)} async-done(((f32[2048,256]{1,0:T(8,128)}), f32[2048,256]{1,0:T(8,128)}) %all-reduce.6.cloned.1.call-update) | async-done | bytes 2097168 | tf_op jit(solution)/shard_map/psum | solution.py:73
  1255.4 2.2 fusion.5
  1257.7 2.9 fusion.7
  (17 shorter events, 0.1 us)
Async XLA Ops:
  7.2 964.4 %all-reduce.4.cloned.1.call-start = ((), (), s32[]{:S(2)}) async-start(), calls=%async_computation | async-start | bytes 2097152 | tf_op jit(solution)/shard_map/psum | solution.py:71
  495.8 23.6 %copy-start.3 = (s32[1024]{0:T(1024)S(1)}, s32[1024]{0:T(1024)}, u32[]{:S(2)}) copy-start(s32[1024]{0:T(1024)} %param.5) | copy-start | bytes 12292
  512.8 299.9 %collective-permute-start = (bf16[1024,2048]{1,0:T(8,128)(2,1)S(1)}, bf16[1024,2048]{1,0:T(8,128)(2,1)}, u32[]{:S(2)}, u32[]{:S(2)}) collective-permute-start(bf16[1024,2048]{1,0:T(8,128)(2,1)S(1)} %multiply_convert_fusion.1), channel_id=1, source_target_pairs={{0,256},{8,264},{16,272},{24,280},{32,288},{40,296},{48,304},{56,3... | collective-permute-start | bytes 12582920 | tf_op jit(solution)/shard_map/ppermute | solution.py:15
  824.2 8.0 copy-start
  830.3 1.9 copy-start.2
  832.2 2.4 copy-start.1
  834.6 420.9 %all-reduce.6.cloned.1.call-start = ((), (), s32[]{:S(2)}) async-start(), calls=%async_computation.1 | async-start | bytes 4194304 | tf_op jit(solution)/shard_map/psum | solution.py:73
Sparse Core Ops, SparseCore 0:
  834.7 136.8 all-reduce.3
  975.6 279.7 all-reduce.5
where the time goes:
time: 1270 us
  waiting for transfers between devices  705 us (56%)
  blocking collectives  469 us (37%)
  other arithmetic  45.9 us (4%)
  between operations  14.2 us (1%)
  matrix products  13.6 us (1%)
  local copies, waits for them, and re-layouts  13.5 us (1%)
    psum x3, blocking collectives, column_scale_of(): return 1.0 / lax.psum(column_part, 'batch')  434 us
    ppermute x1, waiting for transfers between devices, shifted(): return lax.ppermute(value, axis, pairs)  293 us
    psum x1, waiting for transfers between devices, body(): proto_upstream = lax.psum(contract_rows(logit_gradient, views), 'batch')  280 us
    psum x1, waiting for transfers between devices, body(): view_upstream = lax.psum(view_part, 'proto')  132 us
  transfers between devices with their start and end apart: 3, of which 3 were waited for; matrix products, arithmetic and copies ran while one was open for 1% of the time, Pallas kernels for 0%

commit v1 on v0

--- a/solution.py
+++ b/solution.py
@@ -68,7 +68,16 @@
         (estimated_likelihood - centroid_agreement.astype(jnp.float32)) / sharpness_divisor
     ).astype(jnp.bfloat16)
     view_part = jnp.dot(logit_gradient, protos, preferred_element_type=jnp.float32)
-    view_upstream = lax.psum(view_part, "proto")
+
+    def frame_store(local_block):
+        n_peers_all = lax.axis_size("proto")
+        y_new = local_block
+        for k in [dev_i for dev_i in (1, 2, 4, 8, 16) if dev_i < n_peers_all]:
+            r2 = lax.ppermute(y_new, "proto", [(tick, tick ^ k) for tick in range(n_peers_all)])
+            y_new = y_new + r2
+        return y_new
+
+    view_upstream = frame_store(view_part)
     emb_grad = norm_back(view_upstream, view_units, view_scale)
     proto_upstream = lax.psum(contract_rows(logit_gradient, views), "batch")
     proto_grad = norm_back(proto_upstream, proto_units, proto_scale)

time: 1270 us -> 1190 us (0.937)
  waiting for transfers between devices: 705 us -> 624 us
    psum x1 -> x0, waiting for transfers between devices: 132 us -> none  [body(): view_upstream = lax.psum(view_part, 'proto')]
    psum x1, waiting for transfers between devices: 280 us -> 307 us  [body(): proto_upstream = lax.psum(contract_rows(logit_gradient, views), 'batch')]
    ppermute x0 -> x3, waiting for transfers between devices: none -> 23.8 us  [frame_store(): lax.ppermute(y_new, 'proto', [(tick, tick ^ k) for tick in range(n_peers_...]
  transfers between devices with their start and end apart: 3 -> 5, of which waited for: 3 -> 3; matrix products, arithmetic and copies ran while one was open for 1% -> 1% of each run, Pallas kernels for 0% -> 0%
where the time goes in v1:
time: 1190 us
  waiting for transfers between devices  624 us (52%)
  blocking collectives  469 us (39%)
  other arithmetic  43.9 us (4%)
  starting transfers between devices  16.4 us (1%)
  between operations  14.3 us (1%)
  local copies, waits for them, and re-layouts  14.1 us (1%)
    psum x3, blocking collectives, column_scale_of(): return 1.0 / lax.psum(column_part, 'batch')  434 us
    psum x1, waiting for transfers between devices, body(): proto_upstream = lax.psum(contract_rows(logit_gradient, views), 'batch')  307 us
    ppermute x1, waiting for transfers between devices, shifted(): return lax.ppermute(value, axis, pairs)  293 us
    ppermute x3, waiting for transfers between devices, frame_store(): lax.ppermute(y_new, 'proto', [(tick, tick ^ k) for tick in range(n_peers_...  23.8 us
  transfers between devices with their start and end apart: 5, of which 3 were waited for; matrix products, arithmetic and copies ran while one was open for 1% of the time, Pallas kernels for 0%

profile of v1, /device:TPU:2, one launch (start us, length us, event | category | flops | bytes accessed | tf_op | source)
XLA Modules:
  0.0 1191.7 jit_solution(12283345561146257793)
XLA Ops:
  7.2 1.2 copy.5
  8.6 1.6 fusion.8
  10.2 6.4 fusion.4
  16.6 151.9 %psum.57 = f32[2048]{0:T(1024)S(1)} all-reduce(f32[2048]{0:T(1024)S(1)} %get-tuple-element.10), channel_id=1, replica_groups=mesh['batch'=64,'proto'=8] {'batch'}, use_global_device_ids=true, to_apply=%region_5.6 | all-reduce | flops 2048 | bytes 16384 | tf_op jit(solution)/shard_map/psum | solution.py:49
  168.5 5.1 fusion
  173.6 10.0 psum.58
  183.7 4.3 multiply_reduce_fusion.2
  188.0 140.0 %psum.59 = f32[2048]{0:T(1024)S(1)} all-reduce(f32[2048]{0:T(1024)S(1)} %multiply_reduce_fusion.2), channel_id=1, replica_groups=mesh['batch'=64,'proto'=8] {'batch'}, use_global_device_ids=true, to_apply=%region_9.10 | all-reduce | flops 2048 | bytes 16384 | tf_op jit(solution)/shard_map/psum | solution.py:49
  328.0 4.8 multiply_reduce_fusion.1
  332.8 11.9 psum.60
  344.7 4.3 multiply_reduce_fusion
  349.0 142.1 %psum.61 = f32[2048]{0:T(1024)S(1)} all-reduce(f32[2048]{0:T(1024)S(1)} %multiply_reduce_fusion), channel_id=1, replica_groups=mesh['batch'=64,'proto'=8] {'batch'}, use_global_device_ids=true, to_apply=%region_13.14 | all-reduce | flops 2048 | bytes 16384 | tf_op jit(solution)/shard_map/psum | solution.py:49
  491.2 4.8 multiply_reduce_fusion.4
  496.0 12.6 %all-reduce = (f32[1024]{0:T(1024)S(1)}, f32[1024]{0:T(1024)S(1)}) all-reduce(f32[1024]{0:T(1024)S(1)} %multiply_reduce_fusion.4, f32[1024]{0:T(1024)S(1)} %get-tuple-element.4), channel_id=1, replica_groups=mesh['batch'=64,'proto'=8] {'proto'}, use_global_device_ids=true, to_apply=%region_15.16 | all-reduce | flops 2048 | bytes 16384 | tf_op jit(solution)/shard_map/psum | solution.py:60
  508.7 4.4 multiply_convert_fusion.1
  513.0 6.5 collective-permute-start
  519.6 293.0 %collective-permute-done = bf16[1024,2048]{1,0:T(8,128)(2,1)} collective-permute-done((bf16[1024,2048]{1,0:T(8,128)(2,1)S(1)}, bf16[1024,2048]{1,0:T(8,128)(2,1)}, u32[]{:S(2)}, u32[]{:S(2)}) %collective-permute-start) | collective-permute-done | bytes 4194336 | tf_op jit(solution)/shard_map/ppermute | solution.py:15
  812.6 11.6 gather_fusion
  824.2 6.1 multiply_convert_fusion
  830.3 1.4 fusion.20
  831.7 1.9 collective-permute-start.1
  833.6 2.7 fusion.16
  836.4 1.4 add.63
  837.7 5.4 collective-permute-start.2
  843.2 23.8 %collective-permute-done.2 = f32[1024,256]{0,1:T(8,128)S(1)} collective-permute-done((f32[1024,256]{0,1:T(8,128)S(1)}, f32[1024,256]{0,1:T(8,128)S(1)}, u32[]{:S(2)}, u32[]{:S(2)}) %collective-permute-start.2) | collective-permute-done | bytes 1048608 | tf_op jit(solution)/shard_map/ppermute | solution.py:76
  867.1 2.5 collective-permute-start.3
  869.6 307.1 %all-reduce.3.cloned.1.call-done = f32[2048,256]{1,0:T(8,128)} async-done(((f32[2048,256]{1,0:T(8,128)}), f32[2048,256]{1,0:T(8,128)}) %all-reduce.3.cloned.1.call-update) | async-done | bytes 2097168 | tf_op jit(solution)/shard_map/psum | solution.py:82
  1176.7 2.2 fusion.5
  1179.0 2.9 fusion.7
  1181.9 1.5 fusion.12
  1183.3 0.2 fusion.14
  1183.5 1.3 copy.6
  (20 shorter events, 0.5 us)
Async XLA Ops:
  7.2 1169.6 %all-reduce.3.cloned.1.call-start = ((), (), s32[]{:S(2)}) async-start(), calls=%async_computation | async-start | bytes 4194304 | tf_op jit(solution)/shard_map/psum | solution.py:82
  496.0 23.6 %copy-start.1 = (s32[1024]{0:T(1024)S(1)}, s32[1024]{0:T(1024)}, u32[]{:S(2)}) copy-start(s32[1024]{0:T(1024)} %param.5) | copy-start | bytes 12292
  513.0 299.6 %collective-permute-start = (bf16[1024,2048]{1,0:T(8,128)(2,1)S(1)}, bf16[1024,2048]{1,0:T(8,128)(2,1)}, u32[]{:S(2)}, u32[]{:S(2)}) collective-permute-start(bf16[1024,2048]{1,0:T(8,128)(2,1)S(1)} %multiply_convert_fusion.1), channel_id=1, source_target_pairs={{0,256},{8,264},{16,272},{24,280},{32,288},{40,296},{48,304},{56,3... | collective-permute-start | bytes 12582920 | tf_op jit(solution)/shard_map/ppermute | solution.py:15
  824.2 6.1 copy-start
  831.7 4.7 collective-permute-start.1
  837.7 29.2 %collective-permute-start.2 = (f32[1024,256]{0,1:T(8,128)S(1)}, f32[1024,256]{0,1:T(8,128)S(1)}, u32[]{:S(2)}, u32[]{:S(2)}) collective-permute-start(f32[1024,256]{0,1:T(8,128)S(1)} %add.63), channel_id=1, source_target_pairs={{0,2},{1,3},{2,0},{3,1},{4,6},{5,7},{6,4},{7,5},{8,10},{9,11},{10,... | collective-permute-start | bytes 3145736 | tf_op jit(solution)/shard_map/ppermute | solution.py:76
  867.1 314.7 %collective-permute-start.3 = (f32[1024,256]{0,1:T(8,128)S(1)}, f32[1024,256]{0,1:T(8,128)}, u32[]{:S(2)}, u32[]{:S(2)}) collective-permute-start(f32[1024,256]{0,1:T(8,128)S(1)} %add.64), channel_id=1, source_target_pairs={{0,4},{1,5},{2,6},{3,7},{4,0},{5,1},{6,2},{7,3},{8,12},{9,13},{10,... | collective-permute-start | bytes 3145736 | tf_op jit(solution)/shard_map/ppermute | solution.py:76
Sparse Core Ops, SparseCore 0:
  836.5 340.2 all-reduce.2
